TPU v7x, 32 devices: a whole 2x2x4 slice. The times are simulated.
32 devices in a mesh: rep: 4 (over y, x), shard: 8 (over z, core).
Axes of the slice: x: 2, y: 2, z: 4, core: 2. Of those that a mesh axis runs over, the one named last changes fastest.
Arguments:
- tokens: bfloat16 [4096, 768], P(('rep', 'shard')), may hold values from -6 to 6
- segment_ids: int32 [32, 128], P(('rep', 'shard')), may hold values from 0 to 3, never falling along the last dimension, each value on 1 to 64 neighbouring positions
- first_gain: bfloat16 [768], P('shard'), may hold values from 0.5 to 1.5
- first_shift: bfloat16 [768], P('shard'), may hold values from -3 to 3
- qkv_weight: bfloat16 [768, 2304], P('shard'), may hold values from -3 to 3, as said below
- qv_bias: bfloat16 [2, 768], P(None, 'shard'), may hold values from -3 to 3
- proj_weight: bfloat16 [768, 768], P('shard'), may hold values from -0.625 to 0.625
- proj_bias: bfloat16 [768], P('shard'), may hold values from -3 to 3
- second_gain: bfloat16 [768], P('shard'), may hold values from 0.5 to 1.5
- second_shift: bfloat16 [768], P('shard'), may hold values from -3 to 3
- fc_weight: bfloat16 [768, 3072], P('shard'), may hold values from -0.21875 to 0.21875
- fc_bias: bfloat16 [3072], P('shard'), may hold values from -3 to 3
- out_weight: bfloat16 [3072, 768], P('shard'), may hold values from -0.109375 to 0.109375
- out_bias: bfloat16 [768], P('shard'), may hold values from -3 to 3
- cotangent: bfloat16 [4096, 768], P(('rep', 'shard')), may hold values from -6 to 6
Outputs:
- block_output: bfloat16 [4096, 768], P(('rep', 'shard'))
- grad_tokens: float32 [4096, 768], P(('rep', 'shard'))
- grad_first_gain: float32 [768], P('shard')
- grad_first_shift: float32 [768], P('shard')
- grad_qkv_weight: float32 [768, 2304], P('shard')
- grad_qv_bias: float32 [2, 768], P(None, 'shard')
- grad_proj_weight: float32 [768, 768], P('shard')
- grad_proj_bias: float32 [768], P('shard')
- grad_second_gain: float32 [768], P('shard')
- grad_second_shift: float32 [768], P('shard')
- grad_fc_weight: float32 [768, 3072], P('shard')
- grad_fc_bias: float32 [3072], P('shard')
- grad_out_weight: float32 [3072, 768], P('shard')
- grad_out_bias: float32 [768], P('shard')
Inputs may be any that keep to these rules, and one draw needn't show every extreme that they name: `segment_ids`: each row holds 4 runs of equal numbers in rising order, each run 1 to 64 long, one of them exactly 64. `qkv_weight`: columns 0 to 767 project to queries, the next 768 columns to keys, the last 768 columns to values.
All inputs are finite; a program needn't handle non-finite values.
Results may differ from a plain program's by a relative error of at most 0.011.
Values may be sent and summed in bfloat16 or wider, within the bound.
A program may use at most 128 MiB of HBM per device.

v0:
```python
import math
import jax
import jax.numpy as jnp
from jax import lax
from jax.sharding import PartitionSpec as P

D = 768
HEADS = 12
HD = 64
EPSILON = 1e-05


def layer_norm(field, norm_gain, norm_shift):
    center = field - jnp.mean(field, axis=-1, keepdims=True)
    spread = jnp.mean(center * center, axis=-1, keepdims=True)
    return center * lax.rsqrt(spread + EPSILON) * norm_gain + norm_shift


def gelu_tanh(field):
    return jax.nn.gelu(field, approximate=True)


def head_split(matrix):
    return matrix.reshape(matrix.shape[0], HEADS, HD)


def masked_scores(query, keys, segments):
    rows = query.shape[0]
    scores = jnp.einsum(
        "qhd,khd->hqk", head_split(query), head_split(keys), preferred_element_type=jnp.float32
    ) * (1.0 / math.sqrt(HD))
    position = lax.iota(jnp.int32, rows)
    allowed = (segments[:, None] == segments[None, :]) & (position[None, :] <= position[:, None])
    return jnp.where(allowed[None], scores, -1e30)


def attend_forward(query, keys, values, segments):
    rows = query.shape[0]
    scores = masked_scores(query, keys, segments)
    row_max = jnp.max(scores, axis=-1, keepdims=True)
    row_total = jnp.sum(jnp.exp(scores - row_max), axis=-1, keepdims=True)
    logsum = row_max + jnp.log(row_total)
    probs = jnp.exp(scores - logsum).astype(jnp.bfloat16)
    attended = jnp.einsum(
        "hqk,khd->qhd", probs, head_split(values), preferred_element_type=jnp.float32
    )
    return (attended.reshape(rows, D).astype(jnp.bfloat16), logsum)


def attend_backward(query, keys, values, segments, attended, logsum, grad_attended):
    rows = query.shape[0]
    scores = masked_scores(query, keys, segments)
    weights = jnp.exp(scores - logsum)
    grad_heads = head_split(grad_attended)
    grad_values = jnp.einsum(
        "hqk,qhd->khd", weights.astype(jnp.bfloat16), grad_heads, preferred_element_type=jnp.float32
    )
    grad_probs = jnp.einsum(
        "qhd,khd->hqk", grad_heads, head_split(values), preferred_element_type=jnp.float32
    )
    delta = jnp.einsum(
        "qhd,qhd->hq", grad_heads, head_split(attended), preferred_element_type=jnp.float32
    )
    grad_scores = (weights * (grad_probs - delta[..., None]) * (1.0 / math.sqrt(HD))).astype(
        jnp.bfloat16
    )
    grad_query = jnp.einsum(
        "hqk,khd->qhd", grad_scores, head_split(keys), preferred_element_type=jnp.float32
    )
    grad_keys = jnp.einsum(
        "hqk,qhd->khd", grad_scores, head_split(query), preferred_element_type=jnp.float32
    )
    return (grad_query.reshape(rows, D), grad_keys.reshape(rows, D), grad_values.reshape(rows, D))


def per_device(
    tokens,
    segment_ids,
    first_gain,
    first_shift,
    qkv_weight,
    qv_bias,
    proj_weight,
    proj_bias,
    second_gain,
    second_shift,
    fc_weight,
    fc_bias,
    out_weight,
    out_bias,
    cotangent,
):
    low = jnp.bfloat16
    segments = segment_ids[0]
    own_rows = tokens.shape[0]
    shards = lax.axis_size("shard")
    reps = lax.axis_size("rep")
    factor = 1.0 / math.sqrt(own_rows * reps * shards)
    small = jnp.stack(
        [
            first_gain,
            first_shift,
            qv_bias[0],
            qv_bias[1],
            proj_bias,
            second_gain,
            second_shift,
            out_bias,
        ]
    )
    small_full = lax.all_gather(small, "shard", axis=1, tiled=True).astype(jnp.float32)
    gain_one, shift_one, q_bias, v_bias, proj_bias_full, gain_two, shift_two, out_bias_full = (
        small_full[i] for i in range(8)
    )
    qkv_full = lax.all_gather(qkv_weight, "shard", axis=0, tiled=True)
    proj_full = lax.all_gather(proj_weight, "shard", axis=0, tiled=True)
    fc_cols = lax.all_to_all(fc_weight, "shard", split_axis=1, concat_axis=0, tiled=True)
    cot_all = lax.all_gather(cotangent, "shard", axis=0, tiled=True)
    inputs = tokens.astype(jnp.float32)
    normed_f, first_back = jax.vjp(layer_norm, inputs, gain_one, shift_one)
    normed_first = normed_f.astype(low)
    projected = jnp.dot(normed_first, qkv_full, preferred_element_type=jnp.float32)
    query = (projected[:, :D] + q_bias).astype(low)
    keys = projected[:, D : 2 * D].astype(low)
    values = (projected[:, 2 * D :] + v_bias).astype(low)
    attended, logsum = attend_forward(query, keys, values, segments)
    residual = (
        inputs + jnp.dot(attended, proj_full, preferred_element_type=jnp.float32) + proj_bias_full
    )
    cot_f = cotangent.astype(jnp.float32)
    term_out_bias = jnp.sum(cot_f, axis=0) * factor
    normed_s, second_back = jax.vjp(layer_norm, residual, gain_two, shift_two)
    normed_second = normed_s.astype(low)
    normed_all = lax.all_gather(normed_second, "shard", axis=0, tiled=True)
    pre_act = jnp.dot(normed_all, fc_cols, preferred_element_type=jnp.float32) + fc_bias.astype(
        jnp.float32
    )
    activated, gelu_back = jax.vjp(gelu_tanh, pre_act)
    hidden = activated.astype(low)
    grad_hidden = jnp.dot(cot_all, out_weight.T, preferred_element_type=jnp.float32)
    (grad_pre,) = gelu_back(grad_hidden)
    grad_pre_low = grad_pre.astype(low)
    term_fc_bias = jnp.sum(grad_pre, axis=0) * factor
    grad_normed_part = jnp.dot(grad_pre_low, fc_cols.T, preferred_element_type=jnp.float32).astype(
        low
    )
    grad_normed_second = lax.psum_scatter(
        grad_normed_part, "shard", scatter_dimension=0, tiled=True
    ).astype(jnp.float32)
    out_part = jnp.dot(hidden, out_weight, preferred_element_type=jnp.float32).astype(low)
    out_sum = lax.psum_scatter(out_part, "shard", scatter_dimension=0, tiled=True).astype(
        jnp.float32
    )
    result = (residual + out_sum + out_bias_full).astype(low)
    term_out_weight = (
        jnp.dot(hidden.T, cot_all, preferred_element_type=jnp.float32) * factor
    ).astype(low)
    term_fc_weight = (
        jnp.dot(normed_all.T, grad_pre_low, preferred_element_type=jnp.float32) * factor
    ).astype(low)
    out_piece = lax.psum_scatter(term_out_weight, "rep", scatter_dimension=0, tiled=True)
    out_grad = lax.all_gather(out_piece, "rep", axis=0, tiled=True).astype(jnp.float32)
    fc_own = D // (shards * reps)
    fc_rows = term_fc_weight.reshape(shards, reps, fc_own, -1).swapaxes(0, 1).reshape(D, -1)
    fc_piece = lax.psum_scatter(fc_rows, "rep", scatter_dimension=0, tiled=True)
    fc_piece = lax.all_to_all(fc_piece, "shard", split_axis=0, concat_axis=1, tiled=True)
    fc_grad = lax.all_gather(fc_piece, "rep", axis=0, tiled=True).astype(jnp.float32)
    grad_from_norm, second_gain_sum, second_shift_sum = second_back(grad_normed_second)
    grad_residual = cot_f + grad_from_norm
    grad_residual_low = grad_residual.astype(low)
    term_proj_bias = jnp.sum(grad_residual, axis=0) * factor
    term_proj_weight = (
        jnp.dot(attended.T, grad_residual_low, preferred_element_type=jnp.float32) * factor
    ).astype(low)
    grad_attended = jnp.dot(
        grad_residual_low, proj_full.T, preferred_element_type=jnp.float32
    ).astype(low)
    grad_query, grad_keys, grad_values = attend_backward(
        query, keys, values, segments, attended, logsum, grad_attended
    )
    grad_projected = jnp.concatenate([grad_query, grad_keys, grad_values], axis=1).astype(low)
    term_qkv_weight = (
        jnp.dot(normed_first.T, grad_projected, preferred_element_type=jnp.float32) * factor
    ).astype(low)
    grad_normed_first = jnp.dot(grad_projected, qkv_full.T, preferred_element_type=jnp.float32)
    grad_input_norm, first_gain_sum, first_shift_sum = first_back(grad_normed_first)
    grad_inputs = grad_residual + grad_input_norm
    proj_share = lax.psum_scatter(term_proj_weight, "shard", scatter_dimension=0, tiled=True)
    qkv_share = lax.psum_scatter(term_qkv_weight, "shard", scatter_dimension=0, tiled=True)
    proj_piece = lax.psum_scatter(proj_share, "rep", scatter_dimension=0, tiled=True)
    qkv_piece = lax.psum_scatter(qkv_share, "rep", scatter_dimension=0, tiled=True)
    proj_grad = lax.all_gather(proj_piece, "rep", axis=0, tiled=True).astype(jnp.float32)
    qkv_grad = lax.all_gather(qkv_piece, "rep", axis=0, tiled=True).astype(jnp.float32)
    terms = jnp.stack(
        [
            first_gain_sum * factor,
            first_shift_sum * factor,
            jnp.sum(grad_query, axis=0) * factor,
            jnp.sum(grad_values, axis=0) * factor,
            term_proj_bias,
            second_gain_sum * factor,
            second_shift_sum * factor,
            term_out_bias,
        ]
    )
    sums, fc_bias_grad = lax.psum(
        (lax.psum_scatter(terms, "shard", scatter_dimension=1, tiled=True), term_fc_bias), "rep"
    )
    return (
        result,
        grad_inputs,
        sums[0],
        sums[1],
        qkv_grad,
        sums[2:4],
        proj_grad,
        sums[4],
        sums[5],
        sums[6],
        fc_grad,
        fc_bias_grad,
        out_grad,
        sums[7],
    )


def solution(mesh):
    return jax.shard_map(
        per_device,
        mesh=mesh,
        in_specs=(
            P(("rep", "shard"), None),
            P(("rep", "shard"), None),
            P("shard"),
            P("shard"),
            P("shard", None),
            P(None, "shard"),
            P("shard", None),
            P("shard"),
            P("shard"),
            P("shard"),
            P("shard", None),
            P("shard"),
            P("shard", None),
            P("shard"),
            P(("rep", "shard"), None),
        ),
        out_specs=(
            P(("rep", "shard"), None),
            P(("rep", "shard"), None),
            P("shard"),
            P("shard"),
            P("shard", None),
            P(None, "shard"),
            P("shard", None),
            P("shard"),
            P("shard"),
            P("shard"),
            P("shard", None),
            P("shard"),
            P("shard", None),
            P("shard"),
        ),
        check_vma=False,
    )
```

profile of v0, /device:TPU:0, one launch (start us, length us, event | category | flops | bytes accessed | tf_op | source)
XLA Modules:
  0.0 454.6 jit_solution(13503436207554731537)
XLA Ops:
  12.4 14.4 %all-gather = bf16[8,96,8]{1,2,0:T(8,128)(2,1)S(1)} all-gather(bf16[1,96,8]{1,2,0:T(8,128)(2,1)S(1)} %bitcast.120), channel_id=1, replica_groups=mesh['rep'=4,'shard'=8] {'shard'}, dimensions={0}, use_global_device_ids=true | all-gather | bytes 13824 | tf_op jit(solution)/shard_map/all_gather | solution.py:111
  27.9 26.1 %all-gather.6.cloned.1.call-done = bf16[768,2304]{1,0:T(8,128)(2,1)} async-done(((bf16[96,2304]{1,0:T(8,128)(2,1)}), bf16[768,2304]{1,0:T(8,128)(2,1)}) %all-gather.6.cloned.1.call-update) | async-done | bytes 3538960 | tf_op jit(solution)/shard_map/all_gather | solution.py:115
  54.0 2.8 fusion.45
  58.2 19.0 %all-gather.8.cloned.1.call-done = bf16[768,768]{1,0:T(8,128)(2,1)} async-done(((bf16[96,768]{1,0:T(8,128)(2,1)}), bf16[768,768]{1,0:T(8,128)(2,1)}) %all-gather.8.cloned.1.call-update) | async-done | bytes 1179664 | tf_op jit(solution)/shard_map/all_gather | solution.py:116
  80.9 3.5 all-to-all-start
  84.5 30.8 %all-gather.12.cloned.1.call-done = bf16[1024,768]{1,0:T(8,128)(2,1)} async-done(((bf16[128,768]{1,0:T(8,128)(2,1)}), bf16[1024,768]{1,0:T(8,128)(2,1)}) %all-gather.12.cloned.1.call-update) | async-done | bytes 1572880 | tf_op jit(solution)/shard_map/all_gather | solution.py:118
  115.3 3.6 fusion.57
  118.9 22.4 %all-gather.10.cloned.1.call-done = bf16[1024,768]{1,0:T(8,128)(2,1)} async-done(((bf16[128,768]{1,0:T(8,128)(2,1)}), bf16[1024,768]{1,0:T(8,128)(2,1)}) %all-gather.10.cloned.1.call-update) | async-done | bytes 1572880 | tf_op jit(solution)/shard_map/all_gather | solution.py:134
  141.3 5.5 %fusion.50 = (f32[384]{0:T(512)}, bf16[1024,384]{1,0:T(8,128)(2,1)S(1)}, f32[1024,384]{1,0:T(8,128)}) fusion(f32[1024,384]{1,0:T(8,128)} %fusion.57, f32[384]{0:T(512)S(1)} %convert_element_type.105, bf16[1024,768]{1,0:T(8,128)(2,1)} %all-gather.10.cloned.1.call-done, bf16[768,384]{1,0:T(8,128)(2,1)S(1)} %bitcast.112), kind=kOutput, calls=%fused_computation.118 | convolution fusion | flops 612630144 | bytes 6097920 | tf_op jit(solution)/shard_map/dot_general | solution.py:135
  147.7 2.2 convolution_convert_fusion
  150.0 3.8 convolution_convert_fusion.1
  153.9 30.1 %reduce-scatter.18.cloned.1.call-done = bf16[128,768]{1,0:T(8,128)(2,1)} async-done(((bf16[1024,768]{1,0:T(8,128)(2,1)}), bf16[128,768]{1,0:T(8,128)(2,1)}) %reduce-scatter.18.cloned.1.call-update) | async-done | bytes 196624 | tf_op jit(solution)/shard_map/reduce_scatter | solution.py:147
  185.7 1.8 fusion.28
  187.5 30.8 %reduce-scatter.16.cloned.1.call-done = bf16[128,768]{1,0:T(8,128)(2,1)} async-done(((bf16[1024,768]{1,0:T(8,128)(2,1)}), bf16[128,768]{1,0:T(8,128)(2,1)}) %reduce-scatter.16.cloned.1.call-update) | async-done | bytes 196624 | tf_op jit(solution)/shard_map/reduce_scatter | solution.py:151
  218.2 2.5 fusion.52
  222.3 2.4 fusion.6
  230.2 3.0 multiply_convert_fusion
  234.7 3.2 fusion.7
  238.1 3.4 fusion.49
  243.1 10.2 %reduce-scatter.22.cloned.1.call-done = bf16[96,768]{1,0:T(8,128)(2,1)} async-done(((bf16[768,768]{1,0:T(8,128)(2,1)}), bf16[96,768]{1,0:T(8,128)(2,1)}) %reduce-scatter.22.cloned.1.call-update) | async-done | bytes 147472 | tf_op jit(solution)/shard_map/reduce_scatter | solution.py:188
  253.3 26.6 %reduce-scatter.24.cloned.1.call-done = bf16[192,384]{1,0:T(8,128)(2,1)} async-done(((bf16[768,384]{1,0:T(8,128)(2,1)}), bf16[192,384]{1,0:T(8,128)(2,1)}) %reduce-scatter.24.cloned.1.call-update) | async-done | bytes 147472 | tf_op jit(solution)/shard_map/reduce_scatter | solution.py:165
  279.9 4.6 %all-to-all-start.1 = ((bf16[8,24,384]{2,1,0:T(8,128)(2,1)}), bf16[8,24,384]{2,1,0:T(8,128)(2,1)S(1)}, u32[]{:S(2)}, u32[]{:S(2)}) async-start(bf16[8,24,384]{2,1,0:T(8,128)(2,1)} %bitcast.117), calls=%async_computation.6 | async-start | bytes 294912 | tf_op jit(solution)/shard_map/all_to_all | solution.py:166
  284.5 41.6 %reduce-scatter.20.cloned.1.call-done = bf16[96,2304]{1,0:T(8,128)(2,1)} async-done(((bf16[768,2304]{1,0:T(8,128)(2,1)}), bf16[96,2304]{1,0:T(8,128)(2,1)}) %reduce-scatter.20.cloned.1.call-update) | async-done | bytes 442384 | tf_op jit(solution)/shard_map/reduce_scatter | solution.py:189
  326.2 26.9 %reduce-scatter.26.cloned.1.call-done = bf16[96,768]{1,0:T(8,128)(2,1)} async-done(((bf16[384,768]{1,0:T(8,128)(2,1)}), bf16[96,768]{1,0:T(8,128)(2,1)}) %reduce-scatter.26.cloned.1.call-update) | async-done | bytes 147472 | tf_op jit(solution)/shard_map/reduce_scatter | solution.py:161
  353.0 10.2 %all_gather.35 = bf16[384,768]{1,0:T(8,128)(2,1)S(1)} all-gather(bf16[96,768]{1,0:T(8,128)(2,1)} %reduce-scatter.26.cloned.1.call-done), channel_id=1, replica_groups=mesh['rep'=4,'shard'=8] {'rep'}, dimensions={0}, use_global_device_ids=true | all-gather | bytes 737280 | tf_op jit(solution)/shard_map/all_gather | solution.py:162
  364.4 10.5 %all_gather.34 = bf16[96,3072]{1,0:T(8,128)(2,1)S(1)} all-gather(bf16[24,3072]{1,0:T(8,128)(2,1)S(1)} %bitcast.116), channel_id=1, replica_groups=mesh['rep'=4,'shard'=8] {'rep'}, dimensions={0}, use_global_device_ids=true | all-gather | bytes 737280 | tf_op jit(solution)/shard_map/all_gather | solution.py:167
  376.9 9.2 %reduce-scatter.28.cloned.1.call-done = f32[96,8]{1,0:T(8,128)} async-done(((f32[768,8]{1,0:T(8,128)}), f32[96,8]{1,0:T(8,128)}) %reduce-scatter.28.cloned.1.call-update) | async-done | bytes 3088
  387.0 10.5 %all-reduce.2 = (f32[8,96]{1,0:T(8,128)S(1)}, f32[384]{0:T(512)}) all-reduce(f32[8,96]{1,0:T(8,128)S(1)} %copy.93, f32[384]{0:T(512)S(1)} %broadcast_multiply_fusion.8), channel_id=1, replica_groups=mesh['rep'=4,'shard'=8] {'rep'}, use_global_device_ids=true, to_apply=%region_21.22 | all-reduce | flops 1152 | bytes 9216 | tf_op jit(solution)/shard_map/psum | solution.py:206
  398.6 11.6 %reduce-scatter.32.cloned.1.call-done = bf16[24,768]{1,0:T(8,128)(2,1)} async-done(((bf16[96,768]{1,0:T(8,128)(2,1)}), bf16[24,768]{1,0:T(8,128)(2,1)}) %reduce-scatter.32.cloned.1.call-update) | async-done | bytes 36880
  410.2 8.5 %all_gather.33 = bf16[96,768]{1,0:T(8,128)(2,1)S(1)} all-gather(bf16[24,768]{1,0:T(8,128)(2,1)} %reduce-scatter.32.cloned.1.call-done), channel_id=1, replica_groups=mesh['rep'=4,'shard'=8] {'rep'}, dimensions={0}, use_global_device_ids=true | all-gather | bytes 184320 | tf_op jit(solution)/shard_map/all_gather | solution.py:192
  419.5 17.9 %reduce-scatter.30.cloned.1.call-done = bf16[24,2304]{1,0:T(8,128)(2,1)} async-done(((bf16[96,2304]{1,0:T(8,128)(2,1)}), bf16[24,2304]{1,0:T(8,128)(2,1)}) %reduce-scatter.30.cloned.1.call-update) | async-done | bytes 110608
  437.4 9.7 %all_gather.32 = bf16[96,2304]{1,0:T(8,128)(2,1)S(1)} all-gather(bf16[24,2304]{1,0:T(8,128)(2,1)} %reduce-scatter.30.cloned.1.call-done), channel_id=1, replica_groups=mesh['rep'=4,'shard'=8] {'rep'}, dimensions={0}, use_global_device_ids=true | all-gather | bytes 552960 | tf_op jit(solution)/shard_map/all_gather | solution.py:193
  (143 shorter events, 30.8 us)
Async XLA Ops:
  7.2 108.1 %copy-start = (bf16[384,768]{1,0:T(8,128)(2,1)S(1)}, bf16[384,768]{1,0:T(8,128)(2,1)}, u32[]{:S(2)}) copy-start(bf16[384,768]{1,0:T(8,128)(2,1)} %param.27) | copy-start | bytes 1769476
  7.2 46.8 %all-gather.6.cloned.1.call-start = ((), (), s32[]{:S(2)}) async-start(), calls=%async_computation.11 | async-start | bytes 3981312 | tf_op jit(solution)/shard_map/all_gather | solution.py:115
  7.9 69.2 %all-gather.8.cloned.1.call-start = ((), (), s32[]{:S(2)}) async-start(), calls=%async_computation.12 | async-start | bytes 1327104 | tf_op jit(solution)/shard_map/all_gather | solution.py:116
  8.7 106.6 %all-gather.12.cloned.1.call-start = ((), (), s32[]{:S(2)}) async-start(), calls=%async_computation.15 | async-start | bytes 1769472 | tf_op jit(solution)/shard_map/all_gather | solution.py:118
  9.4 131.9 %all-gather.10.cloned.1.call-start = ((), (), s32[]{:S(2)}) async-start(), calls=%async_computation.13 | async-start | bytes 1769472 | tf_op jit(solution)/shard_map/all_gather | solution.py:134
  10.5 46.3 %copy-start.10 = (f32[128]{0:T(128)}, f32[128]{0:T(128)S(1)}, u32[]{:S(2)}) copy-start(f32[128]{0:T(128)S(1)} %broadcast_multiply_fusion.10) | copy-start | bytes 1540
  11.6 45.1 %copy-start.20 = (f32[128]{0:T(128)}, f32[128]{0:T(128)S(1)}, u32[]{:S(2)}) copy-start(f32[128]{0:T(128)S(1)} %fusion.26) | copy-start | bytes 1540
  27.9 28.9 %copy-start.16 = (f32[128]{0:T(128)}, f32[128]{0:T(128)S(1)}, u32[]{:S(2)}) copy-start(f32[128]{0:T(128)S(1)} %fusion.40) | copy-start | bytes 1540
  57.4 19.7 %copy-start.1 = (bf16[128,768]{1,0:T(8,128)(2,1)S(1)}, bf16[128,768]{1,0:T(8,128)(2,1)}, u32[]{:S(2)}) copy-start(bf16[128,768]{1,0:T(8,128)(2,1)} %param.15) | copy-start | bytes 589828
  77.1 2.9 copy-start.9
  79.1 5.3 %copy-start.19 = (bf16[384]{0:T(512)(128)(2,1)S(1)}, bf16[384]{0:T(512)(128)(2,1)}, u32[]{:S(2)}) copy-start(bf16[384]{0:T(512)(128)(2,1)} %param.26) | copy-start | bytes 2308
  80.9 38.0 %all-to-all-start = ((bf16[96,8,384]{2,0,1:T(8,128)(2,1)}), bf16[96,8,384]{2,0,1:T(8,128)(2,1)S(1)}, u32[]{:S(2)}, u32[]{:S(2)}) async-start(bf16[96,8,384]{2,0,1:T(8,128)(2,1)} %bitcast.91), calls=%async_computation | async-start | bytes 1179648 | tf_op jit(solution)/shard_map/all_to_all | solution.py:117
  84.4 99.5 %reduce-scatter.18.cloned.1.call-start = ((), (), s32[]{:S(2)}) async-start(), calls=%async_computation.16 | async-start | bytes 1769472 | tf_op jit(solution)/shard_map/reduce_scatter | solution.py:147
  149.9 68.3 %reduce-scatter.16.cloned.1.call-start = ((), (), s32[]{:S(2)}) async-start(), calls=%async_computation.14 | async-start | bytes 1769472 | tf_op jit(solution)/shard_map/reduce_scatter | solution.py:151
  153.8 64.5 %copy-start.8 = (bf16[128,768]{1,0:T(8,128)(2,1)S(1)}, bf16[128,768]{1,0:T(8,128)(2,1)}, u32[]{:S(2)}) copy-start(bf16[128,768]{1,0:T(8,128)(2,1)} %param.29) | copy-start | bytes 589828
  153.8 99.4 %reduce-scatter.22.cloned.1.call-start = ((), (), s32[]{:S(2)}) async-start(), calls=%async_computation.18 | async-start | bytes 1327104 | tf_op jit(solution)/shard_map/reduce_scatter | solution.py:188
  220.7 1.5 copy-start.23
  222.2 57.7 %reduce-scatter.24.cloned.1.call-start = ((), (), s32[]{:S(2)}) async-start(), calls=%async_computation.19 | async-start | bytes 737280 | tf_op jit(solution)/shard_map/reduce_scatter | solution.py:165
  225.6 100.5 %reduce-scatter.20.cloned.1.call-start = ((), (), s32[]{:S(2)}) async-start(), calls=%async_computation.17 | async-start | bytes 3981312 | tf_op jit(solution)/shard_map/reduce_scatter | solution.py:189
  227.4 1.6 copy-start.6
  227.4 2.0 copy-start.4
  233.3 4.6 %copy-start.12 = (f32[768]{0:T(1024)S(1)}, f32[768]{0:T(1024)}, u32[]{:S(2)}) copy-start(f32[768]{0:T(1024)} %get-tuple-element.20) | copy-start | bytes 9220
  233.3 4.7 %copy-start.13 = (f32[768]{0:T(1024)S(1)}, f32[768]{0:T(1024)}, u32[]{:S(2)}) copy-start(f32[768]{0:T(1024)} %get-tuple-element.14) | copy-start | bytes 9220
  233.3 4.7 %copy-start.14 = (f32[768]{0:T(1024)S(1)}, f32[768]{0:T(1024)}, u32[]{:S(2)}) copy-start(f32[768]{0:T(1024)} %get-tuple-element.34) | copy-start | bytes 9220
  233.3 4.7 %copy-start.15 = (f32[768]{0:T(1024)S(1)}, f32[768]{0:T(1024)}, u32[]{:S(2)}) copy-start(f32[768]{0:T(1024)} %get-tuple-element.43) | copy-start | bytes 9220
  233.3 119.7 %reduce-scatter.26.cloned.1.call-start = ((), (), s32[]{:S(2)}) async-start(), calls=%async_computation.20 | async-start | bytes 737280 | tf_op jit(solution)/shard_map/reduce_scatter | solution.py:161
  237.9 148.2 %reduce-scatter.28.cloned.1.call-start = ((), (), s32[]{:S(2)}) async-start(), calls=%async_computation.21 | async-start | bytes 442368
  238.1 3.6 copy-start.21
  241.5 43.0 %copy-start.18 = (f32[384]{0:T(512)S(1)}, f32[384]{0:T(512)}, u32[]{:S(2)}) copy-start(f32[384]{0:T(512)} %get-tuple-element.32) | copy-start | bytes 4612
  243.0 167.2 %reduce-scatter.32.cloned.1.call-start = ((), (), s32[]{:S(2)}) async-start(), calls=%async_computation.23 | async-start | bytes 184320
  279.9 84.5 %all-to-all-start.1 = ((bf16[8,24,384]{2,1,0:T(8,128)(2,1)}), bf16[8,24,384]{2,1,0:T(8,128)(2,1)S(1)}, u32[]{:S(2)}, u32[]{:S(2)}) async-start(bf16[8,24,384]{2,1,0:T(8,128)(2,1)} %bitcast.117), calls=%async_computation.6 | async-start | bytes 294912 | tf_op jit(solution)/shard_map/all_to_all | solution.py:166
  284.5 152.9 %reduce-scatter.30.cloned.1.call-start = ((), (), s32[]{:S(2)}) async-start(), calls=%async_computation.22 | async-start | bytes 552960
  (7 other events, 8.2 us)
Sparse Core Ops, SparseCore 0:
  9.7 44.2 all-gather.5
  55.6 21.4 all-gather.7
  78.8 36.4 all-gather.11
  117.4 23.8 all-gather.9
  150.0 33.8 reduce-scatter.17
  186.1 32.1 reduce-scatter.15
  222.3 30.8 reduce-scatter.21
  256.7 23.1 reduce-scatter.23
  282.3 43.7 reduce-scatter.19
  329.4 23.5 reduce-scatter.25
  355.4 30.6 reduce-scatter.27
  388.7 21.4 reduce-scatter.31
  413.1 24.2 reduce-scatter.29
where the time goes:
time: 456 us; the launch traced here: 455 us
  waiting for transfers between devices  305 us (67%)
  blocking collectives  63.8 us (14%)
  matrix products  36.5 us (8%)
  other arithmetic  15.5 us (3%)
  between operations  14.5 us (3%)
  local copies, waits for them, and re-layouts  10.1 us (2%)
  starting transfers between devices  8.85 us (2%)
    reduce_scatter x1, waiting for transfers between devices, per_device(): lax.psum_scatter(term_qkv_weight, 'shard', scatter_dimension=0, tiled=True)  41.6 us
    unnamed x16, waiting for transfers between devices  41 us
    all_gather x1, waiting for transfers between devices, per_device(): cot_all = lax.all_gather(cotangent, 'shard', axis=0, tiled=True)  30.8 us
    reduce_scatter x1, waiting for transfers between devices, per_device(): lax.psum_scatter(out_part, 'shard', scatter_dimension=0, tiled=True)  30.8 us
    reduce_scatter x1, waiting for transfers between devices, per_device(): lax.psum_scatter(grad_normed_part, 'shard', scatter_dimension=0, tiled=True)  30.1 us
    reduce_scatter x1, waiting for transfers between devices, per_device(): lax.psum_scatter(term_out_weight, 'rep', scatter_dimension=0, tiled=True)  26.9 us
    reduce_scatter x1, waiting for transfers between devices, per_device(): fc_piece = lax.psum_scatter(fc_rows, 'rep', scatter_dimension=0, tiled=True)  26.6 us
    all_gather x1, waiting for transfers between devices, per_device(): qkv_full = lax.all_gather(qkv_weight, 'shard', axis=0, tiled=True)  26.1 us
  transfers between devices with their start and end apart: 15, of which 13 were waited for; matrix products, arithmetic and copies ran while one was open for 10% of the time, Pallas kernels for 0%

commit v1 on v0

--- a/solution.py
+++ b/solution.py
@@ -115,7 +115,6 @@
     qkv_full = lax.all_gather(qkv_weight, "shard", axis=0, tiled=True)
     proj_full = lax.all_gather(proj_weight, "shard", axis=0, tiled=True)
     fc_cols = lax.all_to_all(fc_weight, "shard", split_axis=1, concat_axis=0, tiled=True)
-    cot_all = lax.all_gather(cotangent, "shard", axis=0, tiled=True)
     inputs = tokens.astype(jnp.float32)
     normed_f, first_back = jax.vjp(layer_norm, inputs, gain_one, shift_one)
     normed_first = normed_f.astype(low)
@@ -131,7 +130,13 @@
     term_out_bias = jnp.sum(cot_f, axis=0) * factor
     normed_s, second_back = jax.vjp(layer_norm, residual, gain_two, shift_two)
     normed_second = normed_s.astype(low)
-    normed_all = lax.all_gather(normed_second, "shard", axis=0, tiled=True)
+    cot_all, normed_all = jnp.split(
+        lax.all_gather(
+            jnp.concatenate([cotangent, normed_second], axis=1), "shard", axis=0, tiled=True
+        ),
+        [cotangent.shape[1]],
+        axis=1,
+    )
     pre_act = jnp.dot(normed_all, fc_cols, preferred_element_type=jnp.float32) + fc_bias.astype(
         jnp.float32
     )

time: 456 us -> 442 us (0.969)
  waiting for transfers between devices: 305 us -> 295 us
    all_gather x2 -> x1, waiting for transfers between devices: 53.2 us -> 14.9 us  [per_device(): lax.all_gather(jnp.concatenate([cotangent, normed_second], axis=1), 'shar...]
    all_to_all x1, waiting for transfers between devices: 0.01 us -> 28.7 us  [per_device(): lax.all_to_all(fc_weight, 'shard', split_axis=1, concat_axis=0, tiled=True)]
    unnamed x16 -> x15, waiting for transfers between devices: 41 us -> 40 us
  transfers between devices with their start and end apart: 15 -> 14, of which waited for: 13 -> 13; matrix products, arithmetic and copies ran while one was open for 10% -> 9% of each run, Pallas kernels for 0% -> 0%
where the time goes in v1:
time: 442 us; the launch traced here: 441 us
  waiting for transfers between devices  295 us (67%)
  blocking collectives  63.8 us (14%)
  matrix products  32.8 us (7%)
  other arithmetic  16.3 us (4%)
  between operations  14.8 us (3%)
  local copies, waits for them, and re-layouts  9.39 us (2%)
  starting transfers between devices  8.83 us (2%)
    reduce_scatter x1, waiting for transfers between devices, per_device(): lax.psum_scatter(term_qkv_weight, 'shard', scatter_dimension=0, tiled=True)  41.6 us
    unnamed x15, waiting for transfers between devices  40 us
    reduce_scatter x1, waiting for transfers between devices, per_device(): lax.psum_scatter(out_part, 'shard', scatter_dimension=0, tiled=True)  30.9 us
    reduce_scatter x1, waiting for transfers between devices, per_device(): lax.psum_scatter(grad_normed_part, 'shard', scatter_dimension=0, tiled=True)  29.2 us
    all_to_all x1, waiting for transfers between devices, per_device(): lax.all_to_all(fc_weight, 'shard', split_axis=1, concat_axis=0, tiled=True)  28.7 us
    reduce_scatter x1, waiting for transfers between devices, per_device(): lax.psum_scatter(term_out_weight, 'rep', scatter_dimension=0, tiled=True)  27 us
    reduce_scatter x1, waiting for transfers between devices, per_device(): fc_piece = lax.psum_scatter(fc_rows, 'rep', scatter_dimension=0, tiled=True)  26.8 us
    all_gather x1, waiting for transfers between devices, per_device(): qkv_full = lax.all_gather(qkv_weight, 'shard', axis=0, tiled=True)  26.3 us
  transfers between devices with their start and end apart: 14, of which 13 were waited for; matrix products, arithmetic and copies ran while one was open for 9% of the time, Pallas kernels for 0%

profile of v1, /device:TPU:0, one launch (start us, length us, event | category | flops | bytes accessed | tf_op | source)
XLA Modules:
  0.0 441.1 jit_solution(860387861600160726)
XLA Ops:
  9.5 14.4 %all-gather = bf16[8,96,8]{1,2,0:T(8,128)(2,1)S(1)} all-gather(bf16[1,96,8]{1,2,0:T(8,128)(2,1)S(1)} %bitcast.116), channel_id=1, replica_groups=mesh['rep'=4,'shard'=8] {'shard'}, dimensions={0}, use_global_device_ids=true | all-gather | bytes 13824 | tf_op jit(solution)/shard_map/all_gather | solution.py:111
  27.6 26.3 %all-gather.5.cloned.1.call-done = bf16[768,2304]{1,0:T(8,128)(2,1)} async-done(((bf16[96,2304]{1,0:T(8,128)(2,1)}), bf16[768,2304]{1,0:T(8,128)(2,1)}) %all-gather.5.cloned.1.call-update) | async-done | bytes 3538960 | tf_op jit(solution)/shard_map/all_gather | solution.py:115
  53.9 2.8 fusion.56
  58.1 19.0 %all-gather.7.cloned.1.call-done = bf16[768,768]{1,0:T(8,128)(2,1)} async-done(((bf16[96,768]{1,0:T(8,128)(2,1)}), bf16[768,768]{1,0:T(8,128)(2,1)}) %all-gather.7.cloned.1.call-update) | async-done | bytes 1179664 | tf_op jit(solution)/shard_map/all_gather | solution.py:116
  81.6 3.5 all-to-all-start
  85.3 28.7 %all-to-all-done = bf16[96,8,384]{2,0,1:T(8,128)(2,1)S(1)} async-done(((bf16[96,8,384]{2,0,1:T(8,128)(2,1)}), bf16[96,8,384]{2,0,1:T(8,128)(2,1)S(1)}, u32[]{:S(2)}, u32[]{:S(2)}) %all-to-all-start) | async-done | bytes 589856 | tf_op jit(solution)/shard_map/all_to_all | solution.py:117
  114.0 14.9 %all-gather.9.cloned.1.call-done = bf16[1024,1536]{1,0:T(8,128)(2,1)} async-done(((bf16[128,1536]{1,0:T(8,128)(2,1)}), bf16[1024,1536]{1,0:T(8,128)(2,1)}) %all-gather.9.cloned.1.call-update) | async-done | bytes 3145744 | tf_op jit(solution)/shard_map/all_gather | solution.py:134
  128.9 2.5 convolution_add_fusion
  131.5 2.4 fusion.66
  134.7 2.2 convolution_convert_fusion
  137.0 3.8 convolution_convert_fusion.1
  140.9 29.2 %reduce-scatter.18.cloned.1.call-done = bf16[128,768]{1,0:T(8,128)(2,1)} async-done(((bf16[1024,768]{1,0:T(8,128)(2,1)}), bf16[128,768]{1,0:T(8,128)(2,1)}) %reduce-scatter.18.cloned.1.call-update) | async-done | bytes 196624 | tf_op jit(solution)/shard_map/reduce_scatter | solution.py:152
  171.8 1.8 fusion.39
  173.7 30.9 %reduce-scatter.16.cloned.1.call-done = bf16[128,768]{1,0:T(8,128)(2,1)} async-done(((bf16[1024,768]{1,0:T(8,128)(2,1)}), bf16[128,768]{1,0:T(8,128)(2,1)}) %reduce-scatter.16.cloned.1.call-update) | async-done | bytes 196624 | tf_op jit(solution)/shard_map/reduce_scatter | solution.py:156
  204.6 2.5 fusion.61
  208.6 2.4 fusion.13
  216.6 3.0 multiply_convert_fusion
  219.7 3.7 fusion.16
  223.5 3.4 fusion.60
  228.6 10.6 %reduce-scatter.22.cloned.1.call-done = bf16[96,768]{1,0:T(8,128)(2,1)} async-done(((bf16[768,768]{1,0:T(8,128)(2,1)}), bf16[96,768]{1,0:T(8,128)(2,1)}) %reduce-scatter.22.cloned.1.call-update) | async-done | bytes 147472 | tf_op jit(solution)/shard_map/reduce_scatter | solution.py:193
  239.3 26.8 %reduce-scatter.24.cloned.1.call-done = bf16[192,384]{1,0:T(8,128)(2,1)} async-done(((bf16[768,384]{1,0:T(8,128)(2,1)}), bf16[192,384]{1,0:T(8,128)(2,1)}) %reduce-scatter.24.cloned.1.call-update) | async-done | bytes 147472 | tf_op jit(solution)/shard_map/reduce_scatter | solution.py:170
  266.1 4.6 %all-to-all-start.1 = ((bf16[8,24,384]{2,1,0:T(8,128)(2,1)}), bf16[8,24,384]{2,1,0:T(8,128)(2,1)S(1)}, u32[]{:S(2)}, u32[]{:S(2)}) async-start(bf16[8,24,384]{2,1,0:T(8,128)(2,1)} %bitcast.113), calls=%async_computation.6 | async-start | bytes 294912 | tf_op jit(solution)/shard_map/all_to_all | solution.py:171
  270.8 41.6 %reduce-scatter.20.cloned.1.call-done = bf16[96,2304]{1,0:T(8,128)(2,1)} async-done(((bf16[768,2304]{1,0:T(8,128)(2,1)}), bf16[96,2304]{1,0:T(8,128)(2,1)}) %reduce-scatter.20.cloned.1.call-update) | async-done | bytes 442384 | tf_op jit(solution)/shard_map/reduce_scatter | solution.py:194
  312.4 27.0 %reduce-scatter.26.cloned.1.call-done = bf16[96,768]{1,0:T(8,128)(2,1)} async-done(((bf16[384,768]{1,0:T(8,128)(2,1)}), bf16[96,768]{1,0:T(8,128)(2,1)}) %reduce-scatter.26.cloned.1.call-update) | async-done | bytes 147472 | tf_op jit(solution)/shard_map/reduce_scatter | solution.py:166
  339.4 10.2 %all_gather.31 = bf16[384,768]{1,0:T(8,128)(2,1)S(1)} all-gather(bf16[96,768]{1,0:T(8,128)(2,1)} %reduce-scatter.26.cloned.1.call-done), channel_id=1, replica_groups=mesh['rep'=4,'shard'=8] {'rep'}, dimensions={0}, use_global_device_ids=true | all-gather | bytes 737280 | tf_op jit(solution)/shard_map/all_gather | solution.py:167
  350.8 10.5 %all_gather.30 = bf16[96,3072]{1,0:T(8,128)(2,1)S(1)} all-gather(bf16[24,3072]{1,0:T(8,128)(2,1)S(1)} %bitcast.112), channel_id=1, replica_groups=mesh['rep'=4,'shard'=8] {'rep'}, dimensions={0}, use_global_device_ids=true | all-gather | bytes 737280 | tf_op jit(solution)/shard_map/all_gather | solution.py:172
  363.3 9.0 %reduce-scatter.28.cloned.1.call-done = f32[96,8]{1,0:T(8,128)} async-done(((f32[768,8]{1,0:T(8,128)}), f32[96,8]{1,0:T(8,128)}) %reduce-scatter.28.cloned.1.call-update) | async-done | bytes 3088
  373.2 10.6 %all-reduce.2 = (f32[8,96]{1,0:T(8,128)S(1)}, f32[384]{0:T(512)}) all-reduce(f32[8,96]{1,0:T(8,128)S(1)} %copy.93, f32[384]{0:T(512)S(1)} %broadcast_multiply_fusion.8), channel_id=1, replica_groups=mesh['rep'=4,'shard'=8] {'rep'}, use_global_device_ids=true, to_apply=%region_21.22 | all-reduce | flops 1152 | bytes 9216 | tf_op jit(solution)/shard_map/psum | solution.py:211
  384.8 11.8 %reduce-scatter.32.cloned.1.call-done = bf16[24,768]{1,0:T(8,128)(2,1)} async-done(((bf16[96,768]{1,0:T(8,128)(2,1)}), bf16[24,768]{1,0:T(8,128)(2,1)}) %reduce-scatter.32.cloned.1.call-update) | async-done | bytes 36880
  396.6 8.5 %all_gather.29 = bf16[96,768]{1,0:T(8,128)(2,1)S(1)} all-gather(bf16[24,768]{1,0:T(8,128)(2,1)} %reduce-scatter.32.cloned.1.call-done), channel_id=1, replica_groups=mesh['rep'=4,'shard'=8] {'rep'}, dimensions={0}, use_global_device_ids=true | all-gather | bytes 184320 | tf_op jit(solution)/shard_map/all_gather | solution.py:197
  405.8 17.7 %reduce-scatter.30.cloned.1.call-done = bf16[24,2304]{1,0:T(8,128)(2,1)} async-done(((bf16[96,2304]{1,0:T(8,128)(2,1)}), bf16[24,2304]{1,0:T(8,128)(2,1)}) %reduce-scatter.30.cloned.1.call-update) | async-done | bytes 110608
  423.6 9.7 %all_gather.28 = bf16[96,2304]{1,0:T(8,128)(2,1)S(1)} all-gather(bf16[24,2304]{1,0:T(8,128)(2,1)} %reduce-scatter.30.cloned.1.call-done), channel_id=1, replica_groups=mesh['rep'=4,'shard'=8] {'rep'}, dimensions={0}, use_global_device_ids=true | all-gather | bytes 552960 | tf_op jit(solution)/shard_map/all_gather | solution.py:198
  (151 shorter events, 30.1 us)
Async XLA Ops:
  7.2 124.2 %copy-start = (bf16[384,768]{1,0:T(8,128)(2,1)S(1)}, bf16[384,768]{1,0:T(8,128)(2,1)}, u32[]{:S(2)}) copy-start(bf16[384,768]{1,0:T(8,128)(2,1)} %param.27) | copy-start | bytes 1769476
  7.2 46.7 %all-gather.5.cloned.1.call-start = ((), (), s32[]{:S(2)}) async-start(), calls=%async_computation.11 | async-start | bytes 3981312 | tf_op jit(solution)/shard_map/all_gather | solution.py:115
  7.9 69.2 %all-gather.7.cloned.1.call-start = ((), (), s32[]{:S(2)}) async-start(), calls=%async_computation.12 | async-start | bytes 1327104 | tf_op jit(solution)/shard_map/all_gather | solution.py:116
  8.7 120.2 %all-gather.9.cloned.1.call-start = ((), (), s32[]{:S(2)}) async-start(), calls=%async_computation.13 | async-start | bytes 3538944 | tf_op jit(solution)/shard_map/all_gather | solution.py:134
  25.0 28.9 %copy-start.10 = (f32[128]{0:T(128)}, f32[128]{0:T(128)S(1)}, u32[]{:S(2)}) copy-start(f32[128]{0:T(128)S(1)} %broadcast_multiply_fusion.10) | copy-start | bytes 1540
  26.8 27.1 %copy-start.23 = (f32[128]{0:T(128)}, f32[128]{0:T(128)S(1)}, u32[]{:S(2)}) copy-start(f32[128]{0:T(128)S(1)} %fusion.37) | copy-start | bytes 1540
  26.8 27.1 %copy-start.18 = (f32[128]{0:T(128)}, f32[128]{0:T(128)S(1)}, u32[]{:S(2)}) copy-start(f32[128]{0:T(128)S(1)} %fusion.51) | copy-start | bytes 1540
  57.4 19.8 %copy-start.1 = (bf16[128,768]{1,0:T(8,128)(2,1)S(1)}, bf16[128,768]{1,0:T(8,128)(2,1)}, u32[]{:S(2)}) copy-start(bf16[128,768]{1,0:T(8,128)(2,1)} %param.15) | copy-start | bytes 589828
  58.1 21.8 %copy-start.7 = (bf16[128,768]{1,0:T(8,128)(2,1)S(1)}, bf16[128,768]{1,0:T(8,128)(2,1)}, u32[]{:S(2)}) copy-start(bf16[128,768]{1,0:T(8,128)(2,1)} %param.29) | copy-start | bytes 589828
  78.9 93.0 %copy-start.17 = (f32[128]{0:T(128)}, f32[128]{0:T(128)S(1)}, u32[]{:S(2)}) copy-start(f32[128]{0:T(128)S(1)} %broadcast_multiply_fusion.9) | copy-start | bytes 1540
  79.1 92.8 %copy-start.20 = (f32[128]{0:T(128)}, f32[128]{0:T(128)S(1)}, u32[]{:S(2)}) copy-start(f32[128]{0:T(128)S(1)} %fusion.52) | copy-start | bytes 1540
  80.7 4.5 %copy-start.22 = (bf16[384]{0:T(512)(128)(2,1)S(1)}, bf16[384]{0:T(512)(128)(2,1)}, u32[]{:S(2)}) copy-start(bf16[384]{0:T(512)(128)(2,1)} %param.26) | copy-start | bytes 2308
  81.6 32.3 %all-to-all-start = ((bf16[96,8,384]{2,0,1:T(8,128)(2,1)}), bf16[96,8,384]{2,0,1:T(8,128)(2,1)S(1)}, u32[]{:S(2)}, u32[]{:S(2)}) async-start(bf16[96,8,384]{2,0,1:T(8,128)(2,1)} %bitcast.87), calls=%async_computation | async-start | bytes 1179648 | tf_op jit(solution)/shard_map/all_to_all | solution.py:117
  85.2 84.9 %reduce-scatter.18.cloned.1.call-start = ((), (), s32[]{:S(2)}) async-start(), calls=%async_computation.15 | async-start | bytes 1769472 | tf_op jit(solution)/shard_map/reduce_scatter | solution.py:152
  128.9 2.6 copy-start.25
  136.9 67.6 %reduce-scatter.16.cloned.1.call-start = ((), (), s32[]{:S(2)}) async-start(), calls=%async_computation.14 | async-start | bytes 1769472 | tf_op jit(solution)/shard_map/reduce_scatter | solution.py:156
  140.8 29.3 %copy-start.9 = (f32[768]{0:T(1024)S(1)}, f32[768]{0:T(1024)}, u32[]{:S(2)}) copy-start(f32[768]{0:T(1024)} %get-tuple-element.24) | copy-start | bytes 9220
  140.8 63.8 %copy-start.12 = (f32[768]{0:T(1024)S(1)}, f32[768]{0:T(1024)}, u32[]{:S(2)}) copy-start(f32[768]{0:T(1024)} %get-tuple-element.22) | copy-start | bytes 9220
  140.8 98.5 %reduce-scatter.22.cloned.1.call-start = ((), (), s32[]{:S(2)}) async-start(), calls=%async_computation.17 | async-start | bytes 1327104 | tf_op jit(solution)/shard_map/reduce_scatter | solution.py:193
  208.6 57.5 %reduce-scatter.24.cloned.1.call-start = ((), (), s32[]{:S(2)}) async-start(), calls=%async_computation.18 | async-start | bytes 737280 | tf_op jit(solution)/shard_map/reduce_scatter | solution.py:170
  212.0 100.4 %reduce-scatter.20.cloned.1.call-start = ((), (), s32[]{:S(2)}) async-start(), calls=%async_computation.16 | async-start | bytes 3981312 | tf_op jit(solution)/shard_map/reduce_scatter | solution.py:194
  219.7 119.8 %reduce-scatter.26.cloned.1.call-start = ((), (), s32[]{:S(2)}) async-start(), calls=%async_computation.19 | async-start | bytes 737280 | tf_op jit(solution)/shard_map/reduce_scatter | solution.py:166
  223.4 3.5 copy-start.24
  223.4 4.1 copy-start.15
  223.4 4.1 copy-start.16
  223.5 4.1 copy-start.14
  223.5 4.1 copy-start.13
  223.5 148.8 %reduce-scatter.28.cloned.1.call-start = ((), (), s32[]{:S(2)}) async-start(), calls=%async_computation.20 | async-start | bytes 442368
  227.0 43.8 %copy-start.21 = (f32[384]{0:T(512)S(1)}, f32[384]{0:T(512)}, u32[]{:S(2)}) copy-start(f32[384]{0:T(512)} %get-tuple-element.55) | copy-start | bytes 4612
  228.6 168.0 %reduce-scatter.32.cloned.1.call-start = ((), (), s32[]{:S(2)}) async-start(), calls=%async_computation.22 | async-start | bytes 184320
  266.1 84.7 %all-to-all-start.1 = ((bf16[8,24,384]{2,1,0:T(8,128)(2,1)}), bf16[8,24,384]{2,1,0:T(8,128)(2,1)S(1)}, u32[]{:S(2)}, u32[]{:S(2)}) async-start(bf16[8,24,384]{2,1,0:T(8,128)(2,1)} %bitcast.113), calls=%async_computation.6 | async-start | bytes 294912 | tf_op jit(solution)/shard_map/all_to_all | solution.py:171
  270.7 152.9 %reduce-scatter.30.cloned.1.call-start = ((), (), s32[]{:S(2)}) async-start(), calls=%async_computation.21 | async-start | bytes 552960
  (11 other events, 15.9 us)
Sparse Core Ops, SparseCore 0:
  9.7 44.2 all-gather.4
  55.6 21.5 all-gather.6
  80.9 47.9 all-gather.8
  137.0 32.9 reduce-scatter.17
  172.2 32.2 reduce-scatter.15
  208.7 30.5 reduce-scatter.21
  242.7 23.3 reduce-scatter.23
  268.5 43.8 reduce-scatter.19
  315.8 23.5 reduce-scatter.25
  341.6 30.6 reduce-scatter.27
  375.1 21.4 reduce-scatter.31
  399.3 24.2 reduce-scatter.29
